TPU v7x, 512 devices: a whole 4x8x8 slice. The times are simulated.
512 devices in a mesh: batch: 32 (over y_lo, x, core), width: 16 (over z, y_hi).
Axes of the slice: x: 4, y: 8 (y_hi: 2, y_lo: 4; y = y_hi * 4 + y_lo), z: 8, core: 2. Of those that a mesh axis runs over, the one named last changes fastest.
Arguments:
- samples: bfloat16 [8192, 8192], P('batch', 'width'), parts along dimension 0, may hold values from -6 to 6
- rank_down: bfloat16 [8192, 2, 1024], P('width'), may hold values from -0.09375 to 0.09375
- rank_up: bfloat16 [1024, 2, 8192], P(None, None, 'width'), may hold values from -0.1875 to 0.1875
- gate_proj: bfloat16 [8192, 2], P('width'), may hold values from -0.0625 to 0.0625
- expert_bias: float32 [2, 8192], P(None, 'width'), may hold values from -3 to 3
Outputs:
- crossed: bfloat16 [8192, 8192], P('batch', 'width'), parts along dimension 0
There are 32 independent parts, one for each index of `batch`. A program takes and returns all parts, laid end to end along the dimension named above; an argument that names none is the same for every part. Nothing has to cross between parts.
All inputs are finite; a program needn't handle non-finite values.
Results may differ from a plain program's by a relative error of at most 0.0027.
Values may be sent and summed in bfloat16 or wider, within the bound.
A program may use at most 64 MiB of HBM per device.

v0:
```python
import jax
import jax.numpy as jnp
from jax import lax
from jax.sharding import PartitionSpec as P


def copy_for_each(array, axis):
    size = lax.axis_size(axis)
    return lax.all_to_all(
        jnp.broadcast_to(array[None], (size, *array.shape)), axis, 0, 0, tiled=True
    )


def taken_together(array, axis):
    everything = copy_for_each(array, axis)
    return jnp.sum(everything, axis=0)


def cut_along(array, dim, size):
    before, after = (array.shape[:dim], array.shape[dim + 1 :])
    return jnp.moveaxis(array.reshape(*before, size, -1, *after), dim, 0)


def sent_and_summed(array, axis, dim):
    pieces = cut_along(array, dim, lax.axis_size(axis))
    arrived = lax.all_to_all(pieces, axis, split_axis=0, concat_axis=0, tiled=True)
    return arrived.sum(axis=0)


def joined_along(pieces, dim):
    pieces = jnp.moveaxis(pieces, 0, dim)
    dims = pieces.shape
    return pieces.reshape(*dims[:dim], dims[dim] * dims[dim + 1], *dims[dim + 2 :])


def gather_directly(array, axis, dim):
    return joined_along(copy_for_each(array, axis), dim)


def shards(samples, rank_down, rank_up, gate_proj, expert_bias):
    expert_count = rank_down.shape[1]
    logits = taken_together(
        jnp.dot(samples, gate_proj, preferred_element_type=jnp.float32), "width"
    )
    gating = jax.nn.sigmoid(logits)
    outputs = []
    for expert_id in range(expert_count):
        down_slab = rank_down[:, expert_id, :]
        up_slab = rank_up[:, expert_id, :]
        shares = sent_and_summed(
            lax.dot_general(
                down_slab, samples, (((0,), (1,)), ((), ())), preferred_element_type=jnp.float32
            ),
            "width",
            0,
        )
        hidden_share = jnp.tanh(shares).astype(jnp.bfloat16)
        outputs.append(
            lax.dot_general(
                gather_directly(hidden_share, "width", 0),
                up_slab,
                (((0,), (0,)), ((), ())),
                preferred_element_type=jnp.float32,
            )
        )
    expanded = jnp.stack(outputs, axis=0)
    blended = jnp.sum(
        jnp.transpose(gating)[:, :, None] * (expanded + expert_bias[:, None, :]), axis=0
    )
    inputs = samples.astype(jnp.float32)
    return (inputs * blended + inputs).astype(jnp.bfloat16)


def solution(mesh):
    placed = (
        P("batch", "width"),
        P("width", None, None),
        P(None, None, "width"),
        P("width", None),
        P(None, "width"),
    )
    return jax.shard_map(
        shards, mesh=mesh, in_specs=placed, out_specs=P("batch", "width"), check_vma=False
    )
```

profile of v0, /device:TPU:44, one launch (start us, length us, event | category | flops | bytes accessed | tf_op | source)
XLA Modules:
  0.0 175.3 jit_solution(5419143972610208378)
XLA Ops:
  0.0 0.0 copy-start
  0.0 0.7 copy-done
  0.7 1.1 fusion.9
  1.8 0.7 broadcast_in_dim.6
  2.4 15.7 %all-to-all-start = ((f32[16,256,2]{1,2,0:T(2,128)}), f32[16,256,2]{1,2,0:T(2,128)S(1)}, u32[]{:S(2)}, u32[]{:S(2)}) async-start(f32[16,256,2]{1,2,0:T(2,128)} %broadcast_in_dim.6), calls=%async_computation | async-start | bytes 65536 | tf_op jit(solution)/shard_map/all_to_all | solution.py:9
  18.1 6.5 %fusion.8 = (bf16[512,1,1024]{2,1,0:T(2,128)(2,1)}, bf16[512,1,1024]{2,1,0:T(2,128)(2,1)S(1)}) fusion(bf16[512,2,1024]{2,1,0:T(2,128)(2,1)} %param.6), kind=kLoop, calls=%fused_computation.17 | loop fusion | bytes 4194304 | tf_op jit(solution)/shard_map/slice | solution.py:48
  24.7 4.6 %copy.26 = bf16[512,1,1024]{0,2,1:T(8,128)(2,1)S(1)} copy(bf16[512,1,1024]{2,1,0:T(2,128)(2,1)} %get-tuple-element.7) | data formatting | bytes 2097152 | tf_op jit(solution)/shard_map/dot_general | solution.py:51
  29.3 0.0 copy-done.2
  29.3 1.5 fusion.5
  30.7 0.0 all-to-all-done
  30.8 12.0 %all-to-all-start.1 = ((f32[16,64,256]{2,1,0:T(8,128)}), f32[16,64,256]{2,1,0:T(8,128)}, u32[]{:S(2)}, u32[]{:S(2)}) async-start(f32[16,64,256]{2,1,0:T(8,128)} %fusion.5), calls=%async_computation.1 | async-start | bytes 2097152 | tf_op jit(solution)/shard_map/all_to_all | solution.py:26
  42.8 2.6 %copy.27 = bf16[512,1,1024]{0,2,1:T(8,128)(2,1)S(1)} copy(bf16[512,1,1024]{2,1,0:T(2,128)(2,1)S(1)} %get-tuple-element.8) | data formatting | bytes 2097152 | tf_op jit(solution)/shard_map/dot_general | solution.py:51
  45.4 1.5 fusion.3
  46.9 34.1 %all-to-all-done.1 = f32[16,64,256]{2,1,0:T(8,128)} async-done(((f32[16,64,256]{2,1,0:T(8,128)}), f32[16,64,256]{2,1,0:T(8,128)}, u32[]{:S(2)}, u32[]{:S(2)}) %all-to-all-start.1) | async-done | bytes 1048608 | tf_op jit(solution)/shard_map/all_to_all | solution.py:26
  81.0 10.2 %all-to-all-start.3 = ((f32[16,64,256]{2,1,0:T(8,128)}), f32[16,64,256]{2,1,0:T(8,128)S(1)}, u32[]{:S(2)}, u32[]{:S(2)}) async-start(f32[16,64,256]{2,1,0:T(8,128)} %fusion.3), calls=%async_computation.3 | async-start | bytes 2097152 | tf_op jit(solution)/shard_map/all_to_all | solution.py:26
  91.2 1.3 reduce_sum.37
  92.5 0.0 copy-start.1
  92.5 28.3 %all-to-all-done.3 = f32[16,64,256]{2,1,0:T(8,128)S(1)} async-done(((f32[16,64,256]{2,1,0:T(8,128)}), f32[16,64,256]{2,1,0:T(8,128)S(1)}, u32[]{:S(2)}, u32[]{:S(2)}) %all-to-all-start.3) | async-done | bytes 1048608 | tf_op jit(solution)/shard_map/all_to_all | solution.py:26
  120.8 0.8 broadcast_in_dim.7
  121.7 10.5 %all-to-all-start.2 = ((bf16[16,64,256]{2,1,0:T(8,128)(2,1)}), bf16[16,64,256]{2,1,0:T(8,128)(2,1)}, u32[]{:S(2)}, u32[]{:S(2)}) async-start(bf16[16,64,256]{2,1,0:T(8,128)(2,1)} %broadcast_in_dim.7), calls=%async_computation.2 | async-start | bytes 1048576 | tf_op jit(solution)/shard_map/all_to_all | solution.py:9
  132.1 0.1 reduce_sum.38
  132.2 16.4 %all-to-all-done.2 = bf16[16,64,256]{2,1,0:T(8,128)(2,1)} async-done(((bf16[16,64,256]{2,1,0:T(8,128)(2,1)}), bf16[16,64,256]{2,1,0:T(8,128)(2,1)}, u32[]{:S(2)}, u32[]{:S(2)}) %all-to-all-start.2) | async-done | bytes 524320 | tf_op jit(solution)/shard_map/all_to_all | solution.py:9
  148.7 0.9 broadcast_in_dim.8
  149.5 7.6 %all-to-all-start.4 = ((bf16[16,64,256]{2,1,0:T(8,128)(2,1)}), bf16[16,64,256]{2,1,0:T(8,128)(2,1)S(1)}, u32[]{:S(2)}, u32[]{:S(2)}) async-start(bf16[16,64,256]{2,1,0:T(8,128)(2,1)} %broadcast_in_dim.8), calls=%async_computation.4 | async-start | bytes 1048576 | tf_op jit(solution)/shard_map/all_to_all | solution.py:9
  157.2 4.2 %fusion.7 = (bf16[1024,1,512]{2,1,0:T(2,128)(2,1)}, bf16[1024,1,512]{2,1,0:T(2,128)(2,1)}) fusion(bf16[1024,2,512]{2,1,0:T(2,128)(2,1)S(1)} %copy-done.1), kind=kLoop, calls=%fused_computation.16 | loop fusion | bytes 4194304 | tf_op jit(solution)/shard_map/slice | solution.py:49
  161.4 2.4 %convolution_bitcast_fusion.1 = f32[1,256,512]{2,1,0:T(8,128)S(1)} fusion(bf16[1024,256]{1,0:T(8,128)(2,1)} %bitcast.5, bf16[1024,1,512]{2,1,0:T(2,128)(2,1)} %get-tuple-element.5), kind=kOutput, calls=%fused_computation.1 | convolution fusion | flops 268435456 | bytes 2097152 | tf_op jit(solution)/shard_map/dot_general | solution.py:59
  163.8 10.1 %all-to-all-done.4 = bf16[16,64,256]{2,1,0:T(8,128)(2,1)S(1)} async-done(((bf16[16,64,256]{2,1,0:T(8,128)(2,1)}), bf16[16,64,256]{2,1,0:T(8,128)(2,1)S(1)}, u32[]{:S(2)}, u32[]{:S(2)}) %all-to-all-start.4) | async-done | bytes 524320 | tf_op jit(solution)/shard_map/all_to_all | solution.py:9
  173.9 0.0 copy-done.3
  173.9 0.5 convolution_bitcast_fusion
  174.3 0.0 copy-done.4
  174.4 0.1 fusion.1
  174.5 0.8 fusion.2
  (8 shorter events, 0.1 us)
Async XLA Ops:
  0.0 0.7 copy-start
  2.4 28.3 %all-to-all-start = ((f32[16,256,2]{1,2,0:T(2,128)}), f32[16,256,2]{1,2,0:T(2,128)S(1)}, u32[]{:S(2)}, u32[]{:S(2)}) async-start(f32[16,256,2]{1,2,0:T(2,128)} %broadcast_in_dim.6), calls=%async_computation | async-start | bytes 65536 | tf_op jit(solution)/shard_map/all_to_all | solution.py:9
  24.7 4.6 %copy-start.2 = (bf16[256,512]{1,0:T(8,128)(2,1)S(1)}, bf16[256,512]{1,0:T(8,128)(2,1)}, u32[]{:S(2)}) copy-start(bf16[256,512]{1,0:T(8,128)(2,1)} %param.5) | copy-start | bytes 786436
  30.8 50.2 %all-to-all-start.1 = ((f32[16,64,256]{2,1,0:T(8,128)}), f32[16,64,256]{2,1,0:T(8,128)}, u32[]{:S(2)}, u32[]{:S(2)}) async-start(f32[16,64,256]{2,1,0:T(8,128)} %fusion.5), calls=%async_computation.1 | async-start | bytes 2097152 | tf_op jit(solution)/shard_map/all_to_all | solution.py:26
  81.0 39.9 %all-to-all-start.3 = ((f32[16,64,256]{2,1,0:T(8,128)}), f32[16,64,256]{2,1,0:T(8,128)S(1)}, u32[]{:S(2)}, u32[]{:S(2)}) async-start(f32[16,64,256]{2,1,0:T(8,128)} %fusion.3), calls=%async_computation.3 | async-start | bytes 2097152 | tf_op jit(solution)/shard_map/all_to_all | solution.py:26
  92.5 64.6 %copy-start.1 = (bf16[1024,2,512]{2,1,0:T(2,128)(2,1)S(1)}, bf16[1024,2,512]{2,1,0:T(2,128)(2,1)}, u32[]{:S(2)}) copy-start(bf16[1024,2,512]{2,1,0:T(2,128)(2,1)} %param.7) | copy-start | bytes 6291460
  121.7 27.0 %all-to-all-start.2 = ((bf16[16,64,256]{2,1,0:T(8,128)(2,1)}), bf16[16,64,256]{2,1,0:T(8,128)(2,1)}, u32[]{:S(2)}, u32[]{:S(2)}) async-start(bf16[16,64,256]{2,1,0:T(8,128)(2,1)} %broadcast_in_dim.7), calls=%async_computation.2 | async-start | bytes 1048576 | tf_op jit(solution)/shard_map/all_to_all | solution.py:9
  149.5 24.3 %all-to-all-start.4 = ((bf16[16,64,256]{2,1,0:T(8,128)(2,1)}), bf16[16,64,256]{2,1,0:T(8,128)(2,1)S(1)}, u32[]{:S(2)}, u32[]{:S(2)}) async-start(bf16[16,64,256]{2,1,0:T(8,128)(2,1)} %broadcast_in_dim.8), calls=%async_computation.4 | async-start | bytes 1048576 | tf_op jit(solution)/shard_map/all_to_all | solution.py:9
  161.3 12.5 %copy-start.3 = (bf16[1024,1,512]{2,1,0:T(2,128)(2,1)S(1)}, bf16[1024,1,512]{2,1,0:T(2,128)(2,1)}, u32[]{:S(2)}) copy-start(bf16[1024,1,512]{2,1,0:T(2,128)(2,1)} %get-tuple-element.6) | copy-start | bytes 3145732
  161.4 12.9 %copy-start.4 = (f32[2,512]{1,0:T(2,128)S(1)}, f32[2,512]{1,0:T(2,128)}, u32[]{:S(2)}) copy-start(f32[2,512]{1,0:T(2,128)} %param.9) | copy-start | bytes 12292
where the time goes:
time: 176 us; the launch traced here: 175 us
  waiting for transfers between devices  88.9 us (51%)
  starting transfers between devices  56.1 us (32%)
  local copies, waits for them, and re-layouts  21 us (12%)
  matrix products  6.86 us (4%)
  other arithmetic  2.36 us (1%)
    all_to_all x2, waiting for transfers between devices, sent_and_summed(): lax.all_to_all(pieces, axis, split_axis=0, concat_axis=0, tiled=True)  62.4 us
    all_to_all x3, starting transfers between devices, copy_for_each(): lax.all_to_all(jnp.broadcast_to(array[None], (size, *array.shape)), axis,...  33.8 us
    all_to_all x3, waiting for transfers between devices, copy_for_each(): lax.all_to_all(jnp.broadcast_to(array[None], (size, *array.shape)), axis,...  26.6 us
    all_to_all x2, starting transfers between devices, sent_and_summed(): lax.all_to_all(pieces, axis, split_axis=0, concat_axis=0, tiled=True)  22.3 us
    dot_general x2, local copies, waits for them, and re-layouts, shards(): lax.dot_general(down_slab, samples, (((0,), (1,)), ((), ())), preferred_e...  7.19 us
    slice x1, local copies, waits for them, and re-layouts, shards(): down_slab = rank_down[:, expert_id, :]  6.54 us
    slice x1, local copies, waits for them, and re-layouts, shards(): up_slab = rank_up[:, expert_id, :]  4.19 us
  transfers between devices with their start and end apart: 5, of which 4 were waited for; matrix products, arithmetic and copies ran while one was open for 14% of the time, Pallas kernels for 0%

commit v1 on v0

v1 whole, which is shorter than its diff:
```python
import functools

import jax
import jax.numpy as jnp
from jax import lax
from jax.experimental import pallas as pl
from jax.experimental.pallas import tpu as pltpu
from jax.sharding import PartitionSpec as P

MESH = pl.DeviceIdType.MESH
BF = jnp.bfloat16
F32 = jnp.float32
RING = 8
PIECES = ((0, 0), (0, 1), (1, 0), (1, 1))
ORDER = (4, 3, -3, 2, -2, 1, -1, 0)
TREES = ((0, 0, 1, 2, 3), (0, 0, 1, 2, 3))


def reach(direction, expert):
    return 4 if (direction == 0) == (expert == 0) else 3


def block(d, distance):
    return ORDER.index(distance if d == 0 or distance in (0, 4) else -distance)


def rows_of(e, h):
    return slice(e * 256 + h * 128, e * 256 + h * 128 + 128)


def kernel(
    x_hbm, w_hbm, u_hbm, gate_hbm, bias_hbm, out_ref,
    x, w, u, gate, bias, xe, part, send, recv, ysend, yrecv, hid, got, logit, lrecv, lsum, lsum_r, acc,
    x_sem, w_sem, u_sem, g_sem, b_sem,
    rs_s, rs_r, y_s, y_r, ag_s, ag_r, l_s, l_r,
):
    me = lax.axis_index("width")
    z = me // 2
    y = lax.rem(me, 2)
    core = lax.rem(lax.axis_index("batch"), 2)

    def at(offset):
        return lax.rem(z + offset + RING, RING)

    def dev(offset):
        return {"width": at(offset) * 2 + y}

    mate = {"width": z * 2 + (1 - y)}

    barrier = pltpu.get_barrier_semaphore()
    x_copy = pltpu.make_async_copy(x_hbm, x, x_sem)
    x_copy.start()
    w_rows = w_hbm.reshape(1024, 1024)
    w_copies = []
    for t, offset in enumerate(ORDER):
        lanes = pl.ds(pl.multiple_of(at(offset) * 128, 128), 128)
        w_copies.append(
            pltpu.make_async_copy(w_rows.at[:, lanes], w.at[:, pl.ds(t * 128, 128)], w_sem.at[t])
        )
        w_copies[-1].start()
    pl.semaphore_signal(barrier, inc=1, device_id=mate, device_id_type=MESH)
    for offset in (1, -1):
        pl.semaphore_signal(barrier, inc=1, device_id=dev(offset), device_id_type=MESH)
    g_copy = pltpu.make_async_copy(gate_hbm, gate, g_sem)
    g_copy.start()
    b_copy = pltpu.make_async_copy(bias_hbm, bias, b_sem)
    b_copy.start()
    u_copy = pltpu.make_async_copy(u_hbm.reshape(2048, 512), u, u_sem)
    u_copy.start()

    row = lax.broadcasted_iota(jnp.int32, (128, 256), 0)
    lane = lax.broadcasted_iota(jnp.int32, (128, 256), 1)
    pick = [jnp.where(lane == 2 * row + e, 1.0, 0.0).astype(BF) for e in range(2)]

    x_copy.wait()
    for e in range(2):
        for c in range(4):
            xe[e * 256 : (e + 1) * 256, c * 256 : (c + 1) * 256] = jnp.dot(
                x[:, c * 128 : (c + 1) * 128], pick[e], preferred_element_type=F32
            ).astype(BF)

    def product(p):
        w_copies[2 * p].wait()
        w_copies[2 * p + 1].wait()
        part[p] = jnp.dot(xe[...], w[:, p * 256 : (p + 1) * 256], preferred_element_type=F32)

    def part_of(t, e, h):
        return part[t // 2, rows_of(e, h), (t % 2) * 128 : (t % 2) * 128 + 128]

    def exchange(tree):
        started = []

        def height(k, n):
            below = [height(c, n) + 1 for c in range(1, n + 1) if tree[c] == k]
            return max(below, default=0)

        def depth(k):
            return 0 if k == 0 else depth(tree[k]) + 1

        def children(k, n):
            return [c for c in range(1, n + 1) if tree[c] == k]

        def rs_copy(d, k, i):
            hop = k - tree[k]
            return pltpu.make_async_remote_copy(
                src_ref=send.at[d, k - 1, i], dst_ref=recv.at[d, k - 1, i],
                send_sem=rs_s.at[d, k - 1, i], recv_sem=rs_r.at[d, k - 1, i],
                device_id=dev(hop if d == 0 else -hop), device_id_type=MESH,
            )

        def rs_sum(d, k, i, value):
            for c in children(k, reach(d, PIECES[i][0])):
                rs_copy(d, c, i).wait_recv()
                value = value + recv[d, c - 1, i].astype(F32)
            return value

        def rs_step(d, k, i):
            e, h = PIECES[i]
            send[d, k - 1, i] = rs_sum(d, k, i, part_of(block(d, k), e, h)).astype(BF)
            copy = rs_copy(d, k, i)
            copy.start()
            started.append(copy)

        def rs_level(level):
            for k in (4, 3, 2, 1):
                for i, (e, h) in enumerate(PIECES):
                    for d in range(2):
                        n = reach(d, e)
                        if k <= n and height(k, n) == level:
                            yield d, k, i

        def l_copy(d, r):
            return pltpu.make_async_remote_copy(
                src_ref=logit if r == 0 else lrecv.at[d, r - 1], dst_ref=lrecv.at[d, r],
                send_sem=l_s.at[d, r], recv_sem=l_r.at[d, r],
                device_id=dev(1 if d == 0 else -1), device_id_type=MESH,
            )

        steps = [list(rs_level(level)) for level in range(4)]
        have = 0
        for level in range(4):
            for d, k, i in steps[level]:
                while have <= block(d, k) // 2:
                    product(have)
                    have += 1
                    if have == 1:
                        pl.semaphore_wait(barrier, 3)
                rs_step(d, k, i)
            if level == 0:
                g_copy.wait()
                logit[...] = lax.dot_general(
                    gate[...], x[...], (((1,), (1,)), ((), ())), preferred_element_type=F32
                )
            for d in range(2 if level < 3 else 1):
                if level > 0:
                    l_copy(d, level - 1).wait_recv()
                copy = l_copy(d, level)
                copy.start()
                started.append(copy)
        while have < 4:
            product(have)
            have += 1

        def y_copy(i):
            return pltpu.make_async_remote_copy(
                src_ref=ysend.at[i], dst_ref=yrecv.at[i], send_sem=y_s.at[i], recv_sem=y_r.at[i],
                device_id=mate, device_id_type=MESH,
            )

        for i, (e, h) in enumerate(PIECES):
            total = part_of(7, e, h)
            for d in (1, 0) if e == 0 else (0, 1):
                total = rs_sum(d, 0, i, total)
            part[3, rows_of(e, h), 128:256] = total
            ysend[i] = total.astype(BF)
            copy = y_copy(i)
            copy.start()
            started.append(copy)

        total = logit[...]
        l_copy(0, 3).wait_recv()
        l_copy(1, 2).wait_recv()
        for d in range(2):
            for r in range(4 - d):
                total = total + lrecv[d, r]
        lsum[...] = total
        l_last = pltpu.make_async_remote_copy(
            src_ref=lsum, dst_ref=lsum_r, send_sem=l_s.at[1, 3], recv_sem=l_r.at[1, 3],
            device_id=mate, device_id_type=MESH,
        )
        l_last.start()
        b_copy.wait()
        for e in range(2):
            acc[e] = jnp.broadcast_to(bias[e : e + 1, :], (256, 512))
        u_copy.wait()

        def ag_copy(d, k, i):
            hop = k - tree[k]
            return pltpu.make_async_remote_copy(
                src_ref=hid.at[i] if tree[k] == 0 else got.at[d, tree[k] - 1, i],
                dst_ref=got.at[d, k - 1, i],
                send_sem=ag_s.at[d, k - 1, i], recv_sem=ag_r.at[d, k - 1, i],
                device_id=dev(hop if d == 0 else -hop), device_id_type=MESH,
            )

        def forward(d, k, i):
            for c in sorted(children(k, reach(d, PIECES[i][0])), reverse=True):
                copy = ag_copy(d, c, i)
                copy.start()
                started.append(copy)

        def expand(values, e, source):
            wide = jnp.dot(values, pick[e], preferred_element_type=F32).astype(BF)
            rows = pl.ds(pl.multiple_of(source * 256, 256), 256)
            acc[e] += jnp.dot(wide, u[rows, :], preferred_element_type=F32)

        for i, (e, h) in enumerate(PIECES):
            y_copy(i).wait_recv()
            hid[i] = jnp.tanh(part[3, rows_of(e, h), 128:256] + yrecv[i].astype(F32)).astype(BF)
            for d in range(2):
                forward(d, 0, i)

        for e in range(2):
            expand(jnp.concatenate([hid[2 * e], hid[2 * e + 1]], axis=0), e, at(0))

        l_last.wait_recv()
        gating = 1.0 / (1.0 + jnp.exp(-(lsum[...] + lsum_r[...])))
        eye = lax.broadcasted_iota(jnp.int32, (128, 128), 0) == lax.broadcasted_iota(
            jnp.int32, (128, 128), 1
        )

        def arrive(level):
            for k in (1, 2, 3, 4):
                if depth(k) != level:
                    continue
                for e in range(2):
                    for d in (0, 1) if e == 0 else (1, 0):
                        if reach(d, e) >= k:
                            for h in range(2):
                                ag_copy(d, k, 2 * e + h).wait_recv()
                                forward(d, k, 2 * e + h)

        def absorb(level):
            for k in (1, 2, 3, 4):
                for e in range(2):
                    for d in (0, 1) if e == 0 else (1, 0):
                        if reach(d, e) >= k and depth(k) == level:
                            expand(
                                jnp.concatenate([got[d, k - 1, 2 * e], got[d, k - 1, 2 * e + 1]], axis=0),
                                e,
                                at(-k if d == 0 else k),
                            )

        for level in range(1, 5):
            arrive(level)
            absorb(level)

        for h in range(2):
            rows = slice(h * 128, h * 128 + 128)
            blended = None
            for e in range(2):
                line = jnp.broadcast_to(gating[e : e + 1, h * 128 : h * 128 + 128], (128, 128))
                column = jnp.sum(jnp.where(eye, line, 0.0), axis=1, keepdims=True)
                term = column * acc[e, rows, :]
                blended = term if blended is None else blended + term
            inputs = x[rows, :].astype(F32)
            out_ref[rows, :] = (inputs * blended + inputs).astype(BF)

        for copy in started:
            copy.wait_send()
        l_last.wait_send()

    if TREES[0] == TREES[1]:
        exchange(TREES[0])
    else:
        for c in range(2):
            pl.when(core == c)(functools.partial(exchange, TREES[c]))


def shards(samples, rank_down, rank_up, gate_proj, expert_bias):
    dma = pltpu.SemaphoreType.DMA
    return pl.pallas_call(
        kernel,
        out_shape=pltpu.VMEM(samples.shape, samples.dtype),
        in_specs=[pl.BlockSpec(memory_space=pl.ANY)] * 5,
        out_specs=pl.BlockSpec(memory_space=pltpu.VMEM),
        scratch_shapes=[
            pltpu.VMEM((256, 512), BF),
            pltpu.VMEM((1024, 1024), BF),
            pltpu.VMEM((2048, 512), BF),
            pltpu.VMEM((2, 512), BF),
            pltpu.VMEM((2, 512), F32),
            pltpu.VMEM((512, 1024), BF),
            pltpu.VMEM((4, 512, 256), F32),
            pltpu.VMEM((2, 4, 4, 128, 128), BF),
            pltpu.VMEM((2, 4, 4, 128, 128), BF),
            pltpu.VMEM((4, 128, 128), BF),
            pltpu.VMEM((4, 128, 128), BF),
            pltpu.VMEM((4, 128, 128), BF),
            pltpu.VMEM((2, 4, 4, 128, 128), BF),
            pltpu.VMEM((2, 256), F32),
            pltpu.VMEM((2, 4, 2, 256), F32),
            pltpu.VMEM((2, 256), F32),
            pltpu.VMEM((2, 256), F32),
            pltpu.VMEM((2, 256, 512), F32),
            dma(()),
            dma((8,)),
            dma(()),
            dma(()),
            dma(()),
            dma((2, 4, 4)),
            dma((2, 4, 4)),
            dma((4,)),
            dma((4,)),
            dma((2, 4, 4)),
            dma((2, 4, 4)),
            dma((2, 4)),
            dma((2, 4)),
        ],
        compiler_params=pltpu.CompilerParams(collective_id=0, has_side_effects=True),
        name="cross_experts",
    )(samples, rank_down, rank_up, gate_proj.T, expert_bias)


def solution(mesh):
    placed = (
        P("batch", "width"),
        P("width", None, None),
        P(None, None, "width"),
        P("width", None),
        P(None, "width"),
    )
    return jax.shard_map(
        shards, mesh=mesh, in_specs=placed, out_specs=P("batch", "width"), check_vma=False
    )
```

time: 176 us -> 48.9 us (0.28)
  the two profiles are of different devices: /device:TPU:44 before, /device:TPU:6 now
where the time goes in v1:
time: 48.9 us; the launch traced here: 48.7 us
  Pallas kernels  48 us (98%)
  local copies, waits for them, and re-layouts  0.71 us (1%)
    pallas_call x1, Pallas kernels, shards(): pl.pallas_call(kernel, out_shape=pltpu.VMEM(samples.shape, samples.dtype)...  48 us

profile of v1, /device:TPU:6, one launch (start us, length us, event | category | flops | bytes accessed | tf_op | source)
XLA Modules:
  0.0 48.7 jit_solution(656058885743965524)
XLA Ops:
  0.0 48.0 %cross_experts.1 = bf16[256,512]{1,0:T(8,128)(2,1)S(1)} custom-call(bf16[256,512]{1,0:T(8,128)(2,1)} %x_hbm.1, bf16[512,2,1024]{2,1,0:T(2,128)(2,1)} %w_hbm.1, bf16[1024,2,512]{2,1,0:T(2,128)(2,1)} %u_hbm.1, bf16[2,512]{1,0:T(2,128)(2,1)} %bitcast.1, f32[2,512]{1,0:T(2,128)} %bias_hbm.1), custom_call_target="tpu_custom_call" | custom-call | tf_op jit(solution)/shard_map/cross_experts/pallas_call | solution.py:282
  48.0 0.7 %copy.7 = bf16[256,512]{1,0:T(8,128)(2,1)} copy(bf16[256,512]{1,0:T(8,128)(2,1)S(1)} %cross_experts.1) | data formatting | bytes 524288

commit v2 on v1

--- a/solution.py
+++ b/solution.py
@@ -11,7 +11,9 @@
 BF = jnp.bfloat16
 F32 = jnp.float32
 RING = 8
-PIECES = ((0, 0), (0, 1), (1, 0), (1, 1))
+CUTS = 2
+TALL = 256 // CUTS
+PIECES = tuple((e, h) for e in range(2) for h in range(CUTS))
 ORDER = (4, 3, -3, 2, -2, 1, -1, 0)
 TREES = ((0, 0, 1, 2, 3), (0, 0, 1, 2, 3))
 
@@ -25,7 +27,12 @@
 
 
 def rows_of(e, h):
-    return slice(e * 256 + h * 128, e * 256 + h * 128 + 128)
+    return slice(e * 256 + h * TALL, e * 256 + h * TALL + TALL)
+
+
+def piece(ref, i):
+    e, h = PIECES[i]
+    return ref.at[e, pl.ds(h * TALL, TALL)]
 
 
 def kernel(
@@ -79,10 +86,14 @@
                 x[:, c * 128 : (c + 1) * 128], pick[e], preferred_element_type=F32
             ).astype(BF)
 
-    def product(p):
-        w_copies[2 * p].wait()
-        w_copies[2 * p + 1].wait()
-        part[p] = jnp.dot(xe[...], w[:, p * 256 : (p + 1) * 256], preferred_element_type=F32)
+    def product(p, e):
+        if e == 0:
+            w_copies[2 * p].wait()
+            w_copies[2 * p + 1].wait()
+        rows = slice(e * 256, e * 256 + 256)
+        part[p, rows, :] = jnp.dot(
+            xe[rows, :], w[:, p * 256 : (p + 1) * 256], preferred_element_type=F32
+        )
 
     def part_of(t, e, h):
         return part[t // 2, rows_of(e, h), (t % 2) * 128 : (t % 2) * 128 + 128]
@@ -103,7 +114,7 @@
         def rs_copy(d, k, i):
             hop = k - tree[k]
             return pltpu.make_async_remote_copy(
-                src_ref=send.at[d, k - 1, i], dst_ref=recv.at[d, k - 1, i],
+                src_ref=piece(send.at[d, k - 1], i), dst_ref=piece(recv.at[d, k - 1], i),
                 send_sem=rs_s.at[d, k - 1, i], recv_sem=rs_r.at[d, k - 1, i],
                 device_id=dev(hop if d == 0 else -hop), device_id_type=MESH,
             )
@@ -111,23 +122,23 @@
         def rs_sum(d, k, i, value):
             for c in children(k, reach(d, PIECES[i][0])):
                 rs_copy(d, c, i).wait_recv()
-                value = value + recv[d, c - 1, i].astype(F32)
+                value = value + piece(recv.at[d, c - 1], i)[...].astype(F32)
             return value
 
         def rs_step(d, k, i):
             e, h = PIECES[i]
-            send[d, k - 1, i] = rs_sum(d, k, i, part_of(block(d, k), e, h)).astype(BF)
+            piece(send.at[d, k - 1], i)[...] = rs_sum(d, k, i, part_of(block(d, k), e, h)).astype(BF)
             copy = rs_copy(d, k, i)
             copy.start()
             started.append(copy)
 
-        def rs_level(level):
+        def rs_round(level, expert):
             for k in (4, 3, 2, 1):
                 for i, (e, h) in enumerate(PIECES):
                     for d in range(2):
                         n = reach(d, e)
-                        if k <= n and height(k, n) == level:
-                            yield d, k, i
+                        if e == expert and k <= n and height(k, n) == level:
+                            rs_step(d, k, i)
 
         def l_copy(d, r):
             return pltpu.make_async_remote_copy(
@@ -136,34 +147,39 @@
                 device_id=dev(1 if d == 0 else -1), device_id_type=MESH,
             )
 
-        steps = [list(rs_level(level)) for level in range(4)]
-        have = 0
-        for level in range(4):
-            for d, k, i in steps[level]:
-                while have <= block(d, k) // 2:
-                    product(have)
-                    have += 1
-                    if have == 1:
-                        pl.semaphore_wait(barrier, 3)
-                rs_step(d, k, i)
-            if level == 0:
-                g_copy.wait()
-                logit[...] = lax.dot_general(
-                    gate[...], x[...], (((1,), (1,)), ((), ())), preferred_element_type=F32
-                )
-            for d in range(2 if level < 3 else 1):
-                if level > 0:
-                    l_copy(d, level - 1).wait_recv()
-                copy = l_copy(d, level)
+        def logit_round(r):
+            for d in range(2 if r < 3 else 1):
+                if r > 0:
+                    l_copy(d, r - 1).wait_recv()
+                copy = l_copy(d, r)
                 copy.start()
                 started.append(copy)
-        while have < 4:
-            product(have)
-            have += 1
+
+        product(0, 0)
+        product(1, 0)
+        pl.semaphore_wait(barrier, 3)
+        rs_round(0, 0)
+        product(0, 1)
+        product(1, 1)
+        product(2, 0)
+        product(2, 1)
+        product(3, 0)
+        product(3, 1)
+        g_copy.wait()
+        logit[...] = lax.dot_general(
+            gate[...], x[...], (((1,), (1,)), ((), ())), preferred_element_type=F32
+        )
+        logit_round(0)
+
+        rs_round(0, 1)
+        for level in range(1, 4):
+            rs_round(level, 0)
+            rs_round(level, 1)
+            logit_round(level)
 
         def y_copy(i):
             return pltpu.make_async_remote_copy(
-                src_ref=ysend.at[i], dst_ref=yrecv.at[i], send_sem=y_s.at[i], recv_sem=y_r.at[i],
+                src_ref=piece(ysend, i), dst_ref=piece(yrecv, i), send_sem=y_s.at[i], recv_sem=y_r.at[i],
                 device_id=mate, device_id_type=MESH,
             )
 
@@ -172,7 +188,7 @@
             for d in (1, 0) if e == 0 else (0, 1):
                 total = rs_sum(d, 0, i, total)
             part[3, rows_of(e, h), 128:256] = total
-            ysend[i] = total.astype(BF)
+            piece(ysend, i)[...] = total.astype(BF)
             copy = y_copy(i)
             copy.start()
             started.append(copy)
@@ -197,8 +213,8 @@
         def ag_copy(d, k, i):
             hop = k - tree[k]
             return pltpu.make_async_remote_copy(
-                src_ref=hid.at[i] if tree[k] == 0 else got.at[d, tree[k] - 1, i],
-                dst_ref=got.at[d, k - 1, i],
+                src_ref=piece(hid if tree[k] == 0 else got.at[d, tree[k] - 1], i),
+                dst_ref=piece(got.at[d, k - 1], i),
                 send_sem=ag_s.at[d, k - 1, i], recv_sem=ag_r.at[d, k - 1, i],
                 device_id=dev(hop if d == 0 else -hop), device_id_type=MESH,
             )
@@ -216,12 +232,13 @@
 
         for i, (e, h) in enumerate(PIECES):
             y_copy(i).wait_recv()
-            hid[i] = jnp.tanh(part[3, rows_of(e, h), 128:256] + yrecv[i].astype(F32)).astype(BF)
+            piece(hid, i)[...] = jnp.tanh(
+                part[3, rows_of(e, h), 128:256] + piece(yrecv, i)[...].astype(F32)
+            ).astype(BF)
             for d in range(2):
                 forward(d, 0, i)
-
-        for e in range(2):
-            expand(jnp.concatenate([hid[2 * e], hid[2 * e + 1]], axis=0), e, at(0))
+            if h == CUTS - 1:
+                expand(hid[e], e, at(0))
 
         l_last.wait_recv()
         gating = 1.0 / (1.0 + jnp.exp(-(lsum[...] + lsum_r[...])))
@@ -229,31 +246,26 @@
             jnp.int32, (128, 128), 1
         )
 
-        def arrive(level):
+        def sources(level, e):
             for k in (1, 2, 3, 4):
-                if depth(k) != level:
-                    continue
-                for e in range(2):
-                    for d in (0, 1) if e == 0 else (1, 0):
-                        if reach(d, e) >= k:
-                            for h in range(2):
-                                ag_copy(d, k, 2 * e + h).wait_recv()
-                                forward(d, k, 2 * e + h)
-
-        def absorb(level):
-            for k in (1, 2, 3, 4):
-                for e in range(2):
-                    for d in (0, 1) if e == 0 else (1, 0):
-                        if reach(d, e) >= k and depth(k) == level:
-                            expand(
-                                jnp.concatenate([got[d, k - 1, 2 * e], got[d, k - 1, 2 * e + 1]], axis=0),
-                                e,
-                                at(-k if d == 0 else k),
-                            )
+                for d in (0, 1) if e == 0 else (1, 0):
+                    if reach(d, e) >= k and depth(k) == level:
+                        yield d, k
+
+        def arrive(level, e):
+            for d, k in sources(level, e):
+                for h in range(CUTS):
+                    ag_copy(d, k, CUTS * e + h).wait_recv()
+                    forward(d, k, CUTS * e + h)
+
+        def absorb(level, e):
+            for d, k in sources(level, e):
+                expand(got[d, k - 1, e], e, at(-k if d == 0 else k))
 
         for level in range(1, 5):
-            arrive(level)
-            absorb(level)
+            for e in range(2):
+                arrive(level, e)
+                absorb(level, e)
 
         for h in range(2):
             rows = slice(h * 128, h * 128 + 128)
@@ -292,12 +304,12 @@
             pltpu.VMEM((2, 512), F32),
             pltpu.VMEM((512, 1024), BF),
             pltpu.VMEM((4, 512, 256), F32),
-            pltpu.VMEM((2, 4, 4, 128, 128), BF),
-            pltpu.VMEM((2, 4, 4, 128, 128), BF),
-            pltpu.VMEM((4, 128, 128), BF),
-            pltpu.VMEM((4, 128, 128), BF),
-            pltpu.VMEM((4, 128, 128), BF),
-            pltpu.VMEM((2, 4, 4, 128, 128), BF),
+            pltpu.VMEM((2, 4, 2, 256, 128), BF),
+            pltpu.VMEM((2, 4, 2, 256, 128), BF),
+            pltpu.VMEM((2, 256, 128), BF),
+            pltpu.VMEM((2, 256, 128), BF),
+            pltpu.VMEM((2, 256, 128), BF),
+            pltpu.VMEM((2, 4, 2, 256, 128), BF),
             pltpu.VMEM((2, 256), F32),
             pltpu.VMEM((2, 4, 2, 256), F32),
             pltpu.VMEM((2, 256), F32),
@@ -308,12 +320,12 @@
             dma(()),
             dma(()),
             dma(()),
-            dma((2, 4, 4)),
-            dma((2, 4, 4)),
-            dma((4,)),
-            dma((4,)),
-            dma((2, 4, 4)),
-            dma((2, 4, 4)),
+            dma((2, 4, 2 * CUTS)),
+            dma((2, 4, 2 * CUTS)),
+            dma((2 * CUTS,)),
+            dma((2 * CUTS,)),
+            dma((2, 4, 2 * CUTS)),
+            dma((2, 4, 2 * CUTS)),
             dma((2, 4)),
             dma((2, 4)),
         ],

time: 48.9 us -> 48.5 us (level)
  no operation moved by 1% of the time
where the time goes in v2:
time: 48.5 us; the launch traced here: 48.3 us
  Pallas kernels  47.6 us (98%)
  local copies, waits for them, and re-layouts  0.71 us (1%)
    pallas_call x1, Pallas kernels, shards(): pl.pallas_call(kernel, out_shape=pltpu.VMEM(samples.shape, samples.dtype)...  47.6 us

profile of v2, /device:TPU:6, one launch (start us, length us, event | category | flops | bytes accessed | tf_op | source)
XLA Modules:
  0.0 48.3 jit_solution(15741151093229579261)
XLA Ops:
  0.0 47.6 %cross_experts.1 = bf16[256,512]{1,0:T(8,128)(2,1)S(1)} custom-call(bf16[256,512]{1,0:T(8,128)(2,1)} %x_hbm.1, bf16[512,2,1024]{2,1,0:T(2,128)(2,1)} %w_hbm.1, bf16[1024,2,512]{2,1,0:T(2,128)(2,1)} %u_hbm.1, bf16[2,512]{1,0:T(2,128)(2,1)} %bitcast.1, f32[2,512]{1,0:T(2,128)} %bias_hbm.1), custom_call_target="tpu_custom_call" | custom-call | tf_op jit(solution)/shard_map/cross_experts/pallas_call | solution.py:294
  47.6 0.7 %copy.7 = bf16[256,512]{1,0:T(8,128)(2,1)} copy(bf16[256,512]{1,0:T(8,128)(2,1)S(1)} %cross_experts.1) | data formatting | bytes 524288

commit v3 on v2

--- a/solution.py
+++ b/solution.py
@@ -37,7 +37,7 @@
 
 def kernel(
     x_hbm, w_hbm, u_hbm, gate_hbm, bias_hbm, out_ref,
-    x, w, u, gate, bias, xe, part, send, recv, ysend, yrecv, hid, got, logit, lrecv, lsum, lsum_r, acc,
+    x, w, u, gate, bias, xe, part, send, recv, ysend, yrecv, hid, got, logit, lrecv, lsum, lsum_r, acc, weight,
     x_sem, w_sem, u_sem, g_sem, b_sem,
     rs_s, rs_r, y_s, y_r, ag_s, ag_r, l_s, l_r,
 ):
@@ -230,6 +230,7 @@
             rows = pl.ds(pl.multiple_of(source * 256, 256), 256)
             acc[e] += jnp.dot(wide, u[rows, :], preferred_element_type=F32)
 
+        early = list(started)
         for i, (e, h) in enumerate(PIECES):
             y_copy(i).wait_recv()
             piece(hid, i)[...] = jnp.tanh(
@@ -266,19 +267,23 @@
             for e in range(2):
                 arrive(level, e)
                 absorb(level, e)
-
-        for h in range(2):
-            rows = slice(h * 128, h * 128 + 128)
-            blended = None
-            for e in range(2):
-                line = jnp.broadcast_to(gating[e : e + 1, h * 128 : h * 128 + 128], (128, 128))
-                column = jnp.sum(jnp.where(eye, line, 0.0), axis=1, keepdims=True)
-                term = column * acc[e, rows, :]
-                blended = term if blended is None else blended + term
-            inputs = x[rows, :].astype(F32)
-            out_ref[rows, :] = (inputs * blended + inputs).astype(BF)
-
-        for copy in started:
+                if level == 2:
+                    for h in range(2):
+                        line = jnp.broadcast_to(gating[e : e + 1, h * 128 : h * 128 + 128], (128, 128))
+                        column = jnp.sum(jnp.where(eye, line, 0.0), axis=1, keepdims=True)
+                        weight[e, h * 128 : h * 128 + 128, :] = jnp.broadcast_to(column, (128, 128))
+            if level == 3:
+                for copy in early:
+                    copy.wait_send()
+
+
+        for c in range(4):
+            lanes = slice(c * 128, c * 128 + 128)
+            blended = weight[0] * acc[0, :, lanes] + weight[1] * acc[1, :, lanes]
+            inputs = x[:, lanes].astype(F32)
+            out_ref[:, lanes] = (inputs * blended + inputs).astype(BF)
+
+        for copy in started[len(early) :]:
             copy.wait_send()
         l_last.wait_send()
 
@@ -315,6 +320,7 @@
             pltpu.VMEM((2, 256), F32),
             pltpu.VMEM((2, 256), F32),
             pltpu.VMEM((2, 256, 512), F32),
+            pltpu.VMEM((2, 256, 128), F32),
             dma(()),
             dma((8,)),
             dma(()),

time: 48.5 us -> 48.4 us (level)
  no operation moved by 1% of the time
where the time goes in v3:
time: 48.4 us; the launch traced here: 48.3 us
  Pallas kernels  47.6 us (98%)
  local copies, waits for them, and re-layouts  0.71 us (1%)
    pallas_call x1, Pallas kernels, shards(): pl.pallas_call(kernel, out_shape=pltpu.VMEM(samples.shape, samples.dtype)...  47.6 us

profile of v3, /device:TPU:6, one launch (start us, length us, event | category | flops | bytes accessed | tf_op | source)
XLA Modules:
  0.0 48.3 jit_solution(17562678271809369665)
XLA Ops:
  0.0 47.6 %cross_experts.1 = bf16[256,512]{1,0:T(8,128)(2,1)S(1)} custom-call(bf16[256,512]{1,0:T(8,128)(2,1)} %x_hbm.1, bf16[512,2,1024]{2,1,0:T(2,128)(2,1)} %w_hbm.1, bf16[1024,2,512]{2,1,0:T(2,128)(2,1)} %u_hbm.1, bf16[2,512]{1,0:T(2,128)(2,1)} %bitcast.1, f32[2,512]{1,0:T(2,128)} %bias_hbm.1), custom_call_target="tpu_custom_call" | custom-call | tf_op jit(solution)/shard_map/cross_experts/pallas_call | solution.py:299
  47.6 0.7 %copy.7 = bf16[256,512]{1,0:T(8,128)(2,1)} copy(bf16[256,512]{1,0:T(8,128)(2,1)S(1)} %cross_experts.1) | data formatting | bytes 524288

commit v4 on v3

--- a/solution.py
+++ b/solution.py
@@ -254,8 +254,8 @@
                         yield d, k
 
         def arrive(level, e):
-            for d, k in sources(level, e):
-                for h in range(CUTS):
+            for h in range(CUTS):
+                for d, k in sources(level, e):
                     ag_copy(d, k, CUTS * e + h).wait_recv()
                     forward(d, k, CUTS * e + h)
 

time: 48.4 us -> 48.5 us (level)
  no operation moved by 1% of the time
where the time goes in v4:
time: 48.5 us; the launch traced here: 48.3 us
  Pallas kernels  47.6 us (98%)
  local copies, waits for them, and re-layouts  0.71 us (1%)
    pallas_call x1, Pallas kernels, shards(): pl.pallas_call(kernel, out_shape=pltpu.VMEM(samples.shape, samples.dtype)...  47.6 us

profile of v4, /device:TPU:6, one launch (start us, length us, event | category | flops | bytes accessed | tf_op | source)
XLA Modules:
  0.0 48.3 jit_solution(4588952321775737737)
XLA Ops:
  0.0 47.6 %cross_experts.1 = bf16[256,512]{1,0:T(8,128)(2,1)S(1)} custom-call(bf16[256,512]{1,0:T(8,128)(2,1)} %x_hbm.1, bf16[512,2,1024]{2,1,0:T(2,128)(2,1)} %w_hbm.1, bf16[1024,2,512]{2,1,0:T(2,128)(2,1)} %u_hbm.1, bf16[2,512]{1,0:T(2,128)(2,1)} %bitcast.1, f32[2,512]{1,0:T(2,128)} %bias_hbm.1), custom_call_target="tpu_custom_call" | custom-call | tf_op jit(solution)/shard_map/cross_experts/pallas_call | solution.py:299
  47.6 0.7 %copy.7 = bf16[256,512]{1,0:T(8,128)(2,1)} copy(bf16[256,512]{1,0:T(8,128)(2,1)S(1)} %cross_experts.1) | data formatting | bytes 524288
